TPU v7x, 32 devices: a whole 2x2x4 slice. The times are simulated.
32 devices in a mesh: pp: 2 (over y), cp: 4 (over z), tp: 4 (over x, core).
Axes of the slice: x: 2, y: 2, z: 4, core: 2. Of those that a mesh axis runs over, the one named last changes fastest.
Arguments:
- query_vectors: bfloat16 [2, 768, 4096], P('pp', 'cp', 'tp'), may hold values from -50 to 50
- key_vectors: bfloat16 [2, 768, 4096], P('pp', 'cp', 'tp'), may hold values from -0.5 to 0.5
- value_vectors: bfloat16 [2, 768, 4096], P('pp', 'cp', 'tp'), may hold values from -150 to 150
- section_inputs: bfloat16 [2, 768, 4096], P('pp', 'cp', 'tp'), may hold values from -6 to 6
- top_grad: bfloat16 [768, 4096], P('cp', 'tp'), may hold values from -6 to 6
- out_gains: float32 [2, 4096], P('pp', 'tp'), may hold values from 0.5 to 2
Outputs:
- section_grads: bfloat16 [2, 768, 4096], P('pp', 'cp', 'tp')
- query_grads: bfloat16 [2, 768, 4096], P('pp', 'cp', 'tp')
- key_grads: bfloat16 [2, 768, 4096], P('pp', 'cp', 'tp')
- value_grads: bfloat16 [2, 768, 4096], P('pp', 'cp', 'tp')
All inputs are finite; a program needn't handle non-finite values.
Results may differ from a plain program's by a relative error of at most 0.01.
Values may be sent and summed in bfloat16 or wider, within the bound.
A program may use at most 64 MiB of HBM per device.

v0:
```python
import jax
import jax.numpy as jnp
from jax import lax
from jax.sharding import PartitionSpec as P

HEAD = 128
WIDTH = 4096


EPSILON = 1e-06


def strict_sum(received, later_side):
    sources = received.shape[0]
    row_ids = lax.broadcasted_iota(jnp.int32, (sources, sources), 0)
    col_ids = lax.broadcasted_iota(jnp.int32, (sources, sources), 1)
    if later_side:
        select = (col_ids > row_ids).astype(jnp.float32)
    else:
        select = (col_ids < row_ids).astype(jnp.float32)
    return jnp.einsum("ij,jrc->irc", select, received, precision=lax.Precision.HIGHEST)


def prefix_exchanged(state):
    shape = state.shape
    sliced = state.reshape(1, shape[0] * shape[1], shape[2])
    summed = strict_sum(
        lax.all_to_all(sliced, "cp", split_axis=1, concat_axis=0, tiled=True), False
    ).astype(jnp.bfloat16)
    result = lax.all_to_all(summed, "cp", split_axis=0, concat_axis=1, tiled=True)
    return result.reshape(shape)


def suffix_exchanged(state):
    shape = state.shape
    sliced = state.reshape(1, shape[0] * shape[1], shape[2])
    summed = strict_sum(
        lax.all_to_all(
            sliced.astype(jnp.bfloat16), "cp", split_axis=1, concat_axis=0, tiled=True
        ).astype(sliced.dtype),
        True,
    ).astype(jnp.bfloat16)
    result = lax.all_to_all(summed, "cp", split_axis=0, concat_axis=1, tiled=True)
    return result.reshape(shape)


def on_device(query_vectors, key_vectors, value_vectors, section_inputs, top_grad, out_gains):
    row_count = query_vectors.shape[1]
    local_width = query_vectors.shape[2]
    head_count = local_width // HEAD
    block_shape = (row_count, head_count, HEAD)
    query_rows = query_vectors[0].reshape(block_shape)
    key_rows = key_vectors[0].reshape(block_shape)
    value_rows = value_vectors[0].reshape(block_shape)
    causal = lax.broadcasted_iota(jnp.int32, (row_count, row_count), 0) >= lax.broadcasted_iota(
        jnp.int32, (row_count, row_count), 1
    )
    local_state = jnp.einsum(
        "thd,the->hde", key_rows, value_rows, preferred_element_type=jnp.float32
    )
    prefix_sum = prefix_exchanged(local_state)
    scores = jnp.where(
        causal,
        jnp.einsum("thd,shd->hts", query_rows, key_rows, preferred_element_type=jnp.float32),
        0.0,
    ).astype(jnp.bfloat16)
    attention = jnp.einsum("hts,she->the", scores, value_rows, preferred_element_type=jnp.float32)
    attention = attention + jnp.einsum(
        "thd,hde->the", query_rows, prefix_sum, preferred_element_type=jnp.float32
    )
    attention = attention.reshape(row_count, local_width)
    squares = lax.psum(jnp.sum(attention * attention, axis=1), "tp")
    scale_root = jnp.sqrt(squares / WIDTH + EPSILON)[:, None]
    normed = attention / scale_root
    sigmoid_gate = jax.nn.sigmoid(section_inputs[0].astype(jnp.float32))
    out_gain = out_gains[0][None, :]
    factor = 1.0 + out_gain * normed * sigmoid_gate * (1.0 - sigmoid_gate)
    own_section = lax.axis_index("pp")
    pieces = lax.all_gather(factor[None], "pp", axis=0, tiled=True)
    section_ids = lax.broadcasted_iota(jnp.int32, (pieces.shape[0], 1, 1), 0)
    later_product = jnp.ones_like(factor) * jnp.prod(
        jnp.where(section_ids > own_section, pieces, 1.0), axis=0
    )
    incoming_grad = top_grad.astype(jnp.float32) * later_product
    section_grad = (incoming_grad * factor).astype(jnp.bfloat16)
    normed_grad = incoming_grad * out_gain * sigmoid_gate
    inner_mean = lax.psum(jnp.sum(normed_grad * normed, axis=1), "tp") / WIDTH
    attention_grad = (
        ((normed_grad - normed * inner_mean[:, None]) / scale_root)
        .astype(jnp.bfloat16)
        .reshape(block_shape)
    )
    grad_state = jnp.einsum(
        "thd,the->hde", query_rows, attention_grad, preferred_element_type=jnp.float32
    )
    suffix_sum = suffix_exchanged(grad_state)
    score_grad = jnp.where(
        causal,
        jnp.einsum("the,she->hts", attention_grad, value_rows, preferred_element_type=jnp.float32),
        0.0,
    ).astype(jnp.bfloat16)
    query_grad = jnp.einsum(
        "hts,shd->thd", score_grad, key_rows, preferred_element_type=jnp.float32
    )
    query_grad = query_grad + jnp.einsum(
        "the,hde->thd", attention_grad, prefix_sum, preferred_element_type=jnp.float32
    )
    key_grad = jnp.einsum(
        "hts,thd->shd", score_grad, query_rows, preferred_element_type=jnp.float32
    )
    key_grad = key_grad + jnp.einsum(
        "she,hde->shd", value_rows, suffix_sum, preferred_element_type=jnp.float32
    )
    value_grad = jnp.einsum(
        "hts,the->she", scores, attention_grad, preferred_element_type=jnp.float32
    )
    value_grad = value_grad + jnp.einsum(
        "shd,hde->she", key_rows, suffix_sum, preferred_element_type=jnp.float32
    )
    query_out = query_grad.reshape(row_count, local_width).astype(jnp.bfloat16)[None]
    key_out = key_grad.reshape(row_count, local_width).astype(jnp.bfloat16)[None]
    value_out = value_grad.reshape(row_count, local_width).astype(jnp.bfloat16)[None]
    return (section_grad[None], query_out, key_out, value_out)


def solution(mesh):
    return jax.shard_map(
        on_device,
        mesh=mesh,
        in_specs=(
            P("pp", "cp", "tp"),
            P("pp", "cp", "tp"),
            P("pp", "cp", "tp"),
            P("pp", "cp", "tp"),
            P("cp", "tp"),
            P("pp", "tp"),
        ),
        out_specs=(
            P("pp", "cp", "tp"),
            P("pp", "cp", "tp"),
            P("pp", "cp", "tp"),
            P("pp", "cp", "tp"),
        ),
        check_vma=False,
    )
```

profile of v0, /device:TPU:0, one launch (start us, length us, event | category | flops | bytes accessed | tf_op | source)
XLA Modules:
  0.0 136.8 jit_solution(17241861988384559180)
XLA Ops:
  7.2 1.1 copy.90
  8.2 1.1 copy.91
  9.4 1.1 fusion.26
  10.5 6.3 %all-to-all-start = ((f32[1,1024,128]{2,0,1:T(1,128)}), f32[1,1024,128]{2,0,1:T(1,128)S(1)}, u32[]{:S(2)}, u32[]{:S(2)}) async-start(f32[1,1024,128]{2,0,1:T(1,128)} %bitcast.4), calls=%async_computation | async-start | bytes 1048576 | tf_op jit(solution)/shard_map/all_to_all | solution.py:28
  17.0 14.4 %all-to-all-done = f32[1,1024,128]{2,0,1:T(1,128)S(1)} async-done(((f32[1,1024,128]{2,0,1:T(1,128)}), f32[1,1024,128]{2,0,1:T(1,128)S(1)}, u32[]{:S(2)}, u32[]{:S(2)}) %all-to-all-start) | async-done | bytes 524320 | tf_op jit(solution)/shard_map/all_to_all | solution.py:28
  31.3 0.9 convolution_convert_fusion.1
  32.2 0.7 copy.62
  33.0 3.4 %all-to-all-start.1 = ((bf16[4,256,128]{2,1,0:T(8,128)(2,1)}), bf16[4,256,128]{2,1,0:T(8,128)(2,1)S(1)}, u32[]{:S(2)}, u32[]{:S(2)}) async-start(bf16[4,256,128]{2,1,0:T(8,128)(2,1)} %copy.62), calls=%async_computation.1 | async-start | bytes 524288 | tf_op jit(solution)/shard_map/all_to_all | solution.py:30
  36.4 0.4 select_convert_fusion.1
  36.8 0.9 copy-done.1
  37.7 0.4 convolution_bitcast_fusion.2
  38.1 6.7 %all-to-all-done.1 = bf16[4,256,128]{2,1,0:T(8,128)(2,1)S(1)} async-done(((bf16[4,256,128]{2,1,0:T(8,128)(2,1)}), bf16[4,256,128]{2,1,0:T(8,128)(2,1)S(1)}, u32[]{:S(2)}, u32[]{:S(2)}) %all-to-all-start.1) | async-done | bytes 262176 | tf_op jit(solution)/shard_map/all_to_all | solution.py:30
  44.8 0.4 multiply_reduce_fusion.1
  45.1 0.3 copy-done.5
  45.5 1.3 copy.64
  46.8 1.3 reshape.157
  48.1 5.7 %psum.14 = f32[192]{0:T(256)S(1)} all-reduce(f32[192]{0:T(256)S(1)} %get-tuple-element.6), channel_id=1, replica_groups=mesh['pp'=2,'cp'=4,'tp'=4] {'tp'}, use_global_device_ids=true, to_apply=%region_1.2 | all-reduce | flops 192 | bytes 1536 | tf_op jit(solution)/shard_map/psum | solution.py:72
  53.8 1.2 multiply_add_fusion
  55.0 26.7 %all-gather.2.cloned.1.call-done = f32[2,192,1024]{2,1,0:T(8,128)} async-done(((f32[1,192,1024]{2,1,0:T(8,128)}), f32[2,192,1024]{2,1,0:T(8,128)}) %all-gather.2.cloned.1.call-update) | async-done | bytes 1572880 | tf_op jit(solution)/shard_map/all_gather | solution.py:79
  81.7 1.7 %select_reduce_fusion = f32[192,1024]{1,0:T(8,128)S(1)} fusion(f32[2,192,1024]{2,1,0:T(8,128)} %all-gather.2.cloned.1.call-done, pred[2]{0:T(512)(128)(4,1)S(1)} %iota_compare_fusion.3), kind=kLoop, calls=%fused_computation.1 | loop fusion | flops 589824 | bytes 2359298 | tf_op jit(solution)/shard_map/reduce_prod | solution.py:81
  83.4 0.4 multiply_reduce_fusion
  83.8 6.4 %psum.15 = f32[192]{0:T(256)S(1)} all-reduce(f32[192]{0:T(256)S(1)} %multiply_reduce_fusion), channel_id=1, replica_groups=mesh['pp'=2,'cp'=4,'tp'=4] {'tp'}, use_global_device_ids=true, to_apply=%region_4.5 | all-reduce | flops 192 | bytes 1536 | tf_op jit(solution)/shard_map/psum | solution.py:87
  90.2 2.4 %fusion.18 = (bf16[24,8,8,128]{3,2,1,0:T(8,128)(2,1)S(1)}, bf16[1,192,1024]{2,1,0:T(8,128)(2,1)}) fusion(f32[192]{0:T(256)S(1)} %add_sqrt_fusion, f32[192]{0:T(256)S(1)} %broadcast_multiply_fusion, f32[1024]{0:T(1024)S(1)} %bitcast.132, f32[192,1024]{1,0:T(8,128)S(1)} %select_reduce_fusion, bf16[192,1024]{1,0:T(8,128)(2,1)} %param.10, ...), kind=kLoop, calls=%fused_computation.41 | loop fusion | flops 3932160 | bytes 3151360
  92.6 0.3 convolution_convert_fusion
  92.9 0.5 fusion.13
  93.4 0.4 copy.146
  93.8 0.5 broadcast.74
  94.4 2.2 %reduce.1 = bf16[1024,128]{1,0:T(8,128)(2,1)S(1)} reduce(bf16[1024,1,128]{2,1,0:T(2,128)(2,1)S(1)} %bitcast.124, bf16[]{:T(256)} %broadcast.74), dimensions={1}, to_apply=%bitcast.107.reduce_sub_computation | reduce | bytes 524290
  96.6 0.8 reshape.165
  97.3 4.6 %all-to-all-start.2 = ((bf16[4,2,16384]{2,1,0:T(2,128)(2,1)}), bf16[4,2,16384]{2,1,0:T(2,128)(2,1)}, u32[]{:S(2)}, u32[]{:S(2)}) async-start(bf16[4,2,16384]{2,1,0:T(2,128)(2,1)} %reshape.165), calls=%async_computation.2 | async-start | bytes 524288 | tf_op jit(solution)/shard_map/all_to_all | solution.py:38
  101.9 0.4 select_convert_fusion
  102.4 0.9 copy-done.3
  103.2 0.4 convolution_bitcast_fusion.1
  103.6 6.6 %all-to-all-done.2 = bf16[4,2,16384]{2,1,0:T(2,128)(2,1)} async-done(((bf16[4,2,16384]{2,1,0:T(2,128)(2,1)}), bf16[4,2,16384]{2,1,0:T(2,128)(2,1)}, u32[]{:S(2)}, u32[]{:S(2)}) %all-to-all-start.2) | async-done | bytes 262176 | tf_op jit(solution)/shard_map/all_to_all | solution.py:38
  110.2 1.9 %reshape.166 = bf16[1024,1,128]{2,1,0:T(2,128)(2,1)} reshape(bf16[4,2,16384]{2,1,0:T(2,128)(2,1)} %all-to-all-done.2) | data formatting | bytes 524288
  112.1 1.1 copy.86
  113.2 0.3 convolution_convert_fusion.2
  113.5 0.7 copy.77
  114.2 4.0 %all-to-all-start.3 = ((bf16[4,256,128]{2,1,0:T(8,128)(2,1)}), bf16[4,256,128]{2,1,0:T(8,128)(2,1)}, u32[]{:S(2)}, u32[]{:S(2)}) async-start(bf16[4,256,128]{2,1,0:T(8,128)(2,1)} %copy.77), calls=%async_computation.3 | async-start | bytes 524288 | tf_op jit(solution)/shard_map/all_to_all | solution.py:43
  118.3 0.3 fusion.3
  118.6 0.3 copy.70
  118.9 0.9 convert_element_type.96
  119.8 0.5 convolution_bitcast_fusion
  120.2 4.9 %all-to-all-done.3 = bf16[4,256,128]{2,1,0:T(8,128)(2,1)} async-done(((bf16[4,256,128]{2,1,0:T(8,128)(2,1)}), bf16[4,256,128]{2,1,0:T(8,128)(2,1)}, u32[]{:S(2)}, u32[]{:S(2)}) %all-to-all-start.3) | async-done | bytes 262176 | tf_op jit(solution)/shard_map/all_to_all | solution.py:43
  125.1 1.2 fusion.6
  126.6 0.9 convert_element_type.105
  127.5 1.3 fusion.4
  129.0 0.9 convert_element_type.102
  (30 shorter events, 0.7 us)
Async XLA Ops:
  8.2 8.6 %copy-start.8 = (bf16[1,192,1024]{2,1,0:T(8,128)(2,1)S(1)}, bf16[1,192,1024]{2,1,0:T(8,128)(2,1)}, u32[]{:S(2)}) copy-start(bf16[1,192,1024]{2,1,0:T(8,128)(2,1)} %param.6) | copy-start | bytes 1179652
  10.5 20.8 %all-to-all-start = ((f32[1,1024,128]{2,0,1:T(1,128)}), f32[1,1024,128]{2,0,1:T(1,128)S(1)}, u32[]{:S(2)}, u32[]{:S(2)}) async-start(f32[1,1024,128]{2,0,1:T(1,128)} %bitcast.4), calls=%async_computation | async-start | bytes 1048576 | tf_op jit(solution)/shard_map/all_to_all | solution.py:28
  16.9 19.9 %copy-start.9 = (pred[192,192]{1,0:T(8,128)(4,1)}, pred[192,192]{1,0:T(8,128)(4,1)S(1)}, u32[]{:S(2)}) copy-start(pred[192,192]{1,0:T(8,128)(4,1)S(1)} %iota_compare_fusion) | copy-start | bytes 110596
  33.0 11.8 %all-to-all-start.1 = ((bf16[4,256,128]{2,1,0:T(8,128)(2,1)}), bf16[4,256,128]{2,1,0:T(8,128)(2,1)S(1)}, u32[]{:S(2)}, u32[]{:S(2)}) async-start(bf16[4,256,128]{2,1,0:T(8,128)(2,1)} %copy.62), calls=%async_computation.1 | async-start | bytes 524288 | tf_op jit(solution)/shard_map/all_to_all | solution.py:30
  36.4 45.3 %all-gather.2.cloned.1.call-start = ((), (), s32[]{:S(2)}) async-start(), calls=%async_computation.4 | async-start | bytes 2359296 | tf_op jit(solution)/shard_map/all_gather | solution.py:79
  36.8 0.9 copy-start.1
  44.8 0.7 copy-start.5
  45.5 8.3 %copy-start = (bf16[1,192,1024]{2,1,0:T(8,128)(2,1)S(1)}, bf16[1,192,1024]{2,1,0:T(8,128)(2,1)}, u32[]{:S(2)}) copy-start(bf16[1,192,1024]{2,1,0:T(8,128)(2,1)} %param.9) | copy-start | bytes 1179652
  45.5 8.3 %copy-start.11 = (f32[1,1024]{1,0:T(1,128)S(1)}, f32[1,1024]{1,0:T(1,128)}, u32[]{:S(2)}) copy-start(f32[1,1024]{1,0:T(1,128)} %param.11) | copy-start | bytes 12292
  55.0 28.4 %copy-start.7 = (bf16[192,1024]{1,0:T(8,128)(2,1)S(1)}, bf16[192,1024]{1,0:T(8,128)(2,1)}, u32[]{:S(2)}) copy-start(bf16[192,1024]{1,0:T(8,128)(2,1)} %param.10) | copy-start | bytes 1179652
  90.2 2.7 %copy-start.2 = (bf16[8,192,192]{2,1,0:T(8,128)(2,1)S(1)}, bf16[8,192,192]{2,1,0:T(8,128)(2,1)}, u32[]{:S(2)}) copy-start(bf16[8,192,192]{2,1,0:T(8,128)(2,1)} %copy-done.1) | copy-start | bytes 1769476
  93.4 8.5 %copy-start.10 = (pred[192,192]{1,0:T(8,128)(4,1)S(1)}, pred[192,192]{1,0:T(8,128)(4,1)}, u32[]{:S(2)}) copy-start(pred[192,192]{1,0:T(8,128)(4,1)} %copy-done.9) | copy-start | bytes 110596
  97.3 12.9 %all-to-all-start.2 = ((bf16[4,2,16384]{2,1,0:T(2,128)(2,1)}), bf16[4,2,16384]{2,1,0:T(2,128)(2,1)}, u32[]{:S(2)}, u32[]{:S(2)}) async-start(bf16[4,2,16384]{2,1,0:T(2,128)(2,1)} %reshape.165), calls=%async_computation.2 | async-start | bytes 524288 | tf_op jit(solution)/shard_map/all_to_all | solution.py:38
  102.4 0.9 copy-start.3
  103.6 14.7 %copy-start.6 = (bf16[4,256,128]{2,1,0:T(8,128)(2,1)S(1)}, bf16[4,256,128]{2,1,0:T(8,128)(2,1)}, u32[]{:S(2)}) copy-start(bf16[4,256,128]{2,1,0:T(8,128)(2,1)} %copy-done.5) | copy-start | bytes 786436
  114.2 10.9 %all-to-all-start.3 = ((bf16[4,256,128]{2,1,0:T(8,128)(2,1)}), bf16[4,256,128]{2,1,0:T(8,128)(2,1)}, u32[]{:S(2)}, u32[]{:S(2)}) async-start(bf16[4,256,128]{2,1,0:T(8,128)(2,1)} %copy.77), calls=%async_computation.3 | async-start | bytes 524288 | tf_op jit(solution)/shard_map/all_to_all | solution.py:43
  118.6 1.2 copy-start.4
Sparse Core Ops, SparseCore 0:
  55.1 26.5 all-gather.1
where the time goes:
time: 138 us; the launch traced here: 137 us
  waiting for transfers between devices  59.2 us (43%)
  starting transfers between devices  18.4 us (13%)
  local copies, waits for them, and re-layouts  16.6 us (12%)
  between operations  14.3 us (10%)
  blocking collectives  12.1 us (9%)
  matrix products  8.22 us (6%)
  other arithmetic  7.95 us (6%)
    all_gather x1, waiting for transfers between devices, on_device(): pieces = lax.all_gather(factor[None], 'pp', axis=0, tiled=True)  26.7 us
    all_to_all x1, waiting for transfers between devices, prefix_exchanged(): lax.all_to_all(sliced, 'cp', split_axis=1, concat_axis=0, tiled=True)  14.4 us
    unnamed x31, local copies, waits for them, and re-layouts  8.58 us
    all_to_all x1, waiting for transfers between devices, prefix_exchanged(): lax.all_to_all(summed, 'cp', split_axis=0, concat_axis=1, tiled=True)  6.69 us
    all_to_all x1, waiting for transfers between devices, suffix_exchanged(): lax.all_to_all(sliced.astype(jnp.bfloat16), 'cp', split_axis=1, concat_ax...  6.62 us
    psum x1, blocking collectives, on_device(): inner_mean = lax.psum(jnp.sum(normed_grad * normed, axis=1), 'tp') / WIDTH  6.39 us
    all_to_all x1, starting transfers between devices, prefix_exchanged(): lax.all_to_all(sliced, 'cp', split_axis=1, concat_axis=0, tiled=True)  6.34 us
    psum x1, blocking collectives, on_device(): squares = lax.psum(jnp.sum(attention * attention, axis=1), 'tp')  5.67 us
  transfers between devices with their start and end apart: 5, of which 5 were waited for; matrix products, arithmetic and copies ran while one was open for 3% of the time, Pallas kernels for 0%

commit v1 on v0

v1 whole, which is shorter than its diff:
```python
import functools

import jax
import jax.numpy as jnp
from jax import lax
from jax.experimental import pallas as pl
from jax.experimental.pallas import tpu as pltpu
from jax.sharding import PartitionSpec as P

HEAD = 128
LANES = 128
EPSILON = 1e-06
MESH = pl.DeviceIdType.MESH
F32 = jnp.float32
BF16 = jnp.bfloat16


def dot(a, b, a_dim, b_dim):
    return lax.dot_general(a, b, (((a_dim,), (b_dim,)), ((), ())), preferred_element_type=F32)


def kernel(
    sizes,
    q_hbm, k_hbm, v_hbm, x_hbm, top_hbm, gain_hbm,
    sec_hbm, qg_hbm, kg_hbm, vg_hbm,
    q, k, v, x, top, gain, sec, qg, kg, vg,
    pre_in, pre_out, suf_in, suf_out, states, scores, att, ng, gate, ag, b_out, b_in,
    rows_out, rows_in, inv_out, inv_in,
    in_sem, sec_sem, out_sem, pre_send, pre_recv, suf_send, suf_recv,
    b_send, b_recv, row_send, row_recv, inv_send, inv_recv,
):
    layers, blocks, shards = sizes
    p, c, t = lax.axis_index("pp"), lax.axis_index("cp"), lax.axis_index("tp")
    rows, width = q.shape
    heads = width // HEAD
    padded = rows_out.shape[2]
    total_width = width * shards

    def cols(h):
        return slice(h * HEAD, (h + 1) * HEAD)

    loads = [
        pltpu.make_async_copy(k_hbm.at[0], k, in_sem.at[0]),
        pltpu.make_async_copy(v_hbm.at[0], v, in_sem.at[1]),
        pltpu.make_async_copy(q_hbm.at[0], q, in_sem.at[2]),
        pltpu.make_async_copy(x_hbm.at[0], x, in_sem.at[3]),
        pltpu.make_async_copy(gain_hbm, gain, in_sem.at[4]),
        pltpu.make_async_copy(top_hbm, top, in_sem.at[5]),
    ]
    for load in loads:
        load.start()

    barrier = pltpu.get_barrier_semaphore()

    @pl.when(c > 0)
    def _():
        pl.semaphore_signal(barrier, inc=1, device_id={"cp": c - 1}, device_id_type=MESH)

    @pl.when(c < blocks - 1)
    def _():
        pl.semaphore_signal(barrier, inc=1, device_id={"cp": c + 1}, device_id_type=MESH)

    for d in range(1, shards):
        pl.semaphore_signal(
            barrier, inc=1, device_id={"tp": lax.rem(t + d, shards)}, device_id_type=MESH
        )
    for d in range(1, layers):
        pl.semaphore_signal(
            barrier, inc=1, device_id={"pp": lax.rem(p + d, layers)}, device_id_type=MESH
        )

    @pl.when(c == 0)
    def _():
        pre_in[...] = jnp.zeros_like(pre_in)

    @pl.when(c == blocks - 1)
    def _():
        suf_in[...] = jnp.zeros_like(suf_in)

    for d in range(1, layers):

        @pl.when(p + d >= layers)
        def _():
            b_in[d - 1] = jnp.zeros(b_in.shape[1:], b_in.dtype)
            inv_in[d - 1] = jnp.zeros(inv_in.shape[1:], inv_in.dtype)

    def pre_copy(h):
        return pltpu.make_async_remote_copy(
            src_ref=pre_out.at[h], dst_ref=pre_in.at[h],
            send_sem=pre_send.at[h], recv_sem=pre_recv.at[h],
            device_id={"cp": c + 1}, device_id_type=MESH,
        )

    def suf_copy(h):
        return pltpu.make_async_remote_copy(
            src_ref=suf_out.at[h], dst_ref=suf_in.at[h],
            send_sem=suf_send.at[h], recv_sem=suf_recv.at[h],
            device_id={"cp": c - 1}, device_id_type=MESH,
        )

    def b_copy(d, h):
        return pltpu.make_async_remote_copy(
            src_ref=b_out.at[h], dst_ref=b_in.at[d - 1, h],
            send_sem=b_send.at[d - 1, h], recv_sem=b_recv.at[d - 1, h],
            device_id={"pp": p - d}, device_id_type=MESH,
        )

    def inv_copy(d):
        return pltpu.make_async_remote_copy(
            src_ref=inv_out, dst_ref=inv_in.at[d - 1],
            send_sem=inv_send.at[d - 1], recv_sem=inv_recv.at[d - 1],
            device_id={"pp": p - d}, device_id_type=MESH,
        )

    def row_copy(i, d):
        return pltpu.make_async_remote_copy(
            src_ref=rows_out.at[i], dst_ref=rows_in.at[i, d - 1],
            send_sem=row_send.at[i, d - 1], recv_sem=row_recv.at[i, d - 1],
            device_id={"tp": lax.rem(t + d, shards)}, device_id_type=MESH,
        )

    def to_row(partial):
        if padded > rows:
            fill = jnp.zeros((padded - rows, LANES), F32)
            partial = jnp.concatenate([partial, fill], axis=0)
        return jnp.broadcast_to(jnp.sum(partial.T, axis=0, keepdims=True), (8, padded))

    def to_col(row):
        return jnp.broadcast_to(row[0:1], (LANES, padded)).T[:rows]

    def row_start(i, partial):
        rows_out[i] = to_row(partial)
        for d in range(1, shards):
            row_copy(i, d).start()

    def row_finish(i):
        total = rows_out[i]
        for d in range(1, shards):
            row_copy(i, d).wait_recv()
            total = total + rows_in[i, d - 1]
        return total

    causal = lax.broadcasted_iota(jnp.int32, (rows, rows), 0) >= lax.broadcasted_iota(
        jnp.int32, (rows, rows), 1
    )
    inner = jnp.logical_and(c > 0, c < blocks - 1)

    partners = (shards - 1) + (layers - 1)
    pl.semaphore_wait(
        barrier, partners + jnp.where(c > 0, 1, 0) + jnp.where(c < blocks - 1, 1, 0)
    )

    loads[0].wait()
    loads[1].wait()
    for h in range(heads):
        state = dot(k[:, cols(h)], v[:, cols(h)], 0, 0)
        states[h] = state
        if blocks > 1:

            @pl.when(c == 0)
            def _():
                pre_out[h] = state.astype(BF16)
                pre_copy(h).start()

    for load in loads[2:5]:
        load.wait()
    squares = jnp.zeros((rows, LANES), F32)
    for h in range(heads):
        query, value = q[:, cols(h)], v[:, cols(h)]
        score = jnp.where(causal, dot(query, k[:, cols(h)], 1, 1), 0.0).astype(BF16)
        scores[h] = score
        attention = dot(score, value, 1, 0)
        sig = jax.nn.sigmoid(x[:, cols(h)].astype(F32))
        gate[:, cols(h)] = sig

        if blocks > 1:

            @pl.when(c > 0)
            def _():
                pre_copy(h).wait_recv()

            @pl.when(inner)
            def _():
                pre_out[h] = (pre_in[h].astype(F32) + states[h]).astype(BF16)
                pre_copy(h).start()

        attention = attention + dot(query, pre_in[h], 1, 0)
        att[:, cols(h)] = attention
        squares = squares + attention * attention
        if layers > 1:
            b_out[h] = (attention * (gain[:, cols(h)] * sig * (1.0 - sig))).astype(BF16)
            for d in range(1, layers):

                @pl.when(p >= d)
                def _():
                    b_copy(d, h).start()

    row_start(0, squares)
    loads[5].wait()
    inv_row = 1.0 / jnp.sqrt(row_finish(0) / total_width + EPSILON)
    inv_out[...] = inv_row
    for d in range(1, layers):

        @pl.when(p >= d)
        def _():
            inv_copy(d).start()

    inv = to_col(inv_row)
    for d in range(1, layers):

        @pl.when(p + d < layers)
        def _():
            inv_copy(d).wait_recv()

    later_inv = [to_col(inv_in[d - 1]) for d in range(1, layers)]
    products = jnp.zeros((rows, LANES), F32)
    for h in range(heads):
        normed = att[:, cols(h)] * inv
        sig = gate[:, cols(h)]
        scaled = gain[:, cols(h)] * sig
        factor = 1.0 + normed * scaled * (1.0 - sig)
        incoming = top[:, cols(h)].astype(F32)
        for d in range(1, layers):

            @pl.when(p + d < layers)
            def _():
                b_copy(d, h).wait_recv()

            incoming = incoming * (1.0 + b_in[d - 1, h].astype(F32) * later_inv[d - 1])
        sec[:, cols(h)] = (incoming * factor).astype(BF16)
        normed_grad = incoming * scaled
        ng[:, cols(h)] = normed_grad
        att[:, cols(h)] = normed
        products = products + normed_grad * normed

    row_start(1, products)
    sec_copy = pltpu.make_async_copy(sec, sec_hbm.at[0], sec_sem)
    sec_copy.start()
    mean = to_col(row_finish(1) / total_width)
    for h in range(heads):
        grad = ((ng[:, cols(h)] - att[:, cols(h)] * mean) * inv).astype(BF16)
        ag[:, cols(h)] = grad
        state = dot(q[:, cols(h)], grad, 0, 0)
        states[h] = state
        if blocks > 1:

            @pl.when(c == blocks - 1)
            def _():
                suf_out[h] = state.astype(BF16)
                suf_copy(h).start()

    def out_copies(h):
        return [
            pltpu.make_async_copy(
                src.at[:, cols(h)], dst.at[0, :, cols(h)], out_sem.at[i, h]
            )
            for i, (src, dst) in enumerate(((qg, qg_hbm), (kg, kg_hbm), (vg, vg_hbm)))
        ]

    for h in range(heads):
        query, key, value = q[:, cols(h)], k[:, cols(h)], v[:, cols(h)]
        grad = ag[:, cols(h)]
        score_grad = jnp.where(causal, dot(grad, value, 1, 1), 0.0).astype(BF16)
        query_grad = dot(score_grad, key, 1, 0) + dot(grad, pre_in[h], 1, 1)
        qg[:, cols(h)] = query_grad.astype(BF16)
        key_grad = dot(score_grad, query, 0, 0)
        value_grad = dot(scores[h], grad, 0, 0)
        if blocks > 1:

            @pl.when(c < blocks - 1)
            def _():
                suf_copy(h).wait_recv()

            @pl.when(inner)
            def _():
                suf_out[h] = (suf_in[h].astype(F32) + states[h]).astype(BF16)
                suf_copy(h).start()

        suffix = suf_in[h]
        kg[:, cols(h)] = (key_grad + dot(value, suffix, 1, 1)).astype(BF16)
        vg[:, cols(h)] = (value_grad + dot(key, suffix, 1, 0)).astype(BF16)
        for copy in out_copies(h):
            copy.start()

    if blocks > 1:

        @pl.when(c < blocks - 1)
        def _():
            for h in range(heads):
                pre_copy(h).wait_send()

        @pl.when(c > 0)
        def _():
            for h in range(heads):
                suf_copy(h).wait_send()

    for d in range(1, layers):

        @pl.when(p >= d)
        def _():
            inv_copy(d).wait_send()
            for h in range(heads):
                b_copy(d, h).wait_send()

    for i in range(2):
        for d in range(1, shards):
            row_copy(i, d).wait_send()
    sec_copy.wait()
    for h in range(heads):
        for copy in out_copies(h):
            copy.wait()


def on_device(sizes, q, k, v, x, top, gains):
    layers, blocks, shards = sizes
    rows, width = q.shape[1:]
    heads = width // HEAD
    padded = -(-rows // LANES) * LANES
    others, peers = max(layers - 1, 1), max(shards - 1, 1)
    wide = pltpu.VMEM((rows, width), BF16)
    wide32 = pltpu.VMEM((rows, width), F32)
    square = pltpu.VMEM((heads, HEAD, HEAD), BF16)
    dma = pltpu.SemaphoreType.DMA
    out = jax.ShapeDtypeStruct((1, rows, width), BF16)
    return pl.pallas_call(
        functools.partial(kernel, sizes),
        out_shape=(out,) * 4,
        in_specs=[pl.BlockSpec(memory_space=pl.ANY)] * 6,
        out_specs=(pl.BlockSpec(memory_space=pl.ANY),) * 4,
        scratch_shapes=[
            wide, wide, wide, wide, wide, pltpu.VMEM((1, width), F32),
            wide, wide, wide, wide,
            square, square, square, square,
            pltpu.VMEM((heads, HEAD, HEAD), F32),
            pltpu.VMEM((heads, rows, rows), BF16),
            wide32, wide32, wide32, wide,
            pltpu.VMEM((heads, rows, HEAD), BF16),
            pltpu.VMEM((others, heads, rows, HEAD), BF16),
            pltpu.VMEM((2, 8, padded), F32),
            pltpu.VMEM((2, peers, 8, padded), F32),
            pltpu.VMEM((8, padded), F32),
            pltpu.VMEM((others, 8, padded), F32),
            dma((6,)), dma, dma((3, heads)),
            dma((heads,)), dma((heads,)), dma((heads,)), dma((heads,)),
            dma((others, heads)), dma((others, heads)),
            dma((2, peers)), dma((2, peers)),
            dma((others,)), dma((others,)),
        ],
        compiler_params=pltpu.CompilerParams(collective_id=0, has_side_effects=True),
    )(q, k, v, x, top, gains)


def solution(mesh):
    sizes = (mesh.shape["pp"], mesh.shape["cp"], mesh.shape["tp"])
    part = P("pp", "cp", "tp")
    return jax.shard_map(
        functools.partial(on_device, sizes),
        mesh=mesh,
        in_specs=(part, part, part, part, P("cp", "tp"), P("pp", "tp")),
        out_specs=(part, part, part, part),
        check_vma=False,
    )
```

time: 138 us -> 47.7 us (0.35)
  waiting for transfers between devices: 59.2 us -> 0 us
  Pallas kernels: 0 us -> 42 us
  starting transfers between devices: 18.4 us -> 0 us
  between operations: 14.3 us -> 0.65 us
  blocking collectives: 12.1 us -> 0 us
  local copies, waits for them, and re-layouts: 16.6 us -> 4.84 us
  matrix products: 8.22 us -> 0 us
  other arithmetic: 7.95 us -> 0 us
    pallas_call x0 -> x1, Pallas kernels: none -> 42 us  [on_device(): pl.pallas_call(functools.partial(kernel, sizes), out_shape=(out,) * 4, in...]
    all_to_all x4 -> x0, waiting for transfers between devices: 32.5 us -> none  [the longest x1 14.4 us: prefix_exchanged(): lax.all_to_all(sliced, 'cp', split_axis=1, concat_axis=0, tiled=True)]
    all_gather x1 -> x0, waiting for transfers between devices: 26.7 us -> none  [on_device(): pieces = lax.all_gather(factor[None], 'pp', axis=0, tiled=True)]
    all_to_all x4 -> x0, starting transfers between devices: 18.4 us -> none  [the longest x1 6.34 us: prefix_exchanged(): lax.all_to_all(sliced, 'cp', split_axis=1, concat_axis=0, tiled=True)]
    psum x2 -> x0, blocking collectives: 12.1 us -> none  [the longest x1 6.39 us: on_device(): inner_mean = lax.psum(jnp.sum(normed_grad * normed, axis=1), 'tp') / WIDTH]
    dot_general x14 -> x0, matrix products: 8.22 us -> none  [the longest x1 1.25 us: on_device(): jnp.einsum('she,hde->shd', value_rows, suffix_sum, preferred_element_type...]
    convert_element_type x9 -> x0, local copies, waits for them, and re-layouts: 5.4 us -> none  [the longest x2 1.17 us: on_device(): query_grad.reshape(row_count, local_width).astype(jnp.bfloat16)[None]]
    unnamed x2 -> x0, other arithmetic: 4.57 us -> none
  transfers between devices with their start and end apart: 5 -> 0, of which waited for: 5 -> 0; matrix products, arithmetic and copies ran while one was open for 3% -> 0% of each run, Pallas kernels for 0% -> 0%
where the time goes in v1:
time: 47.7 us; the launch traced here: 47.5 us
  Pallas kernels  42 us (88%)
  local copies, waits for them, and re-layouts  4.84 us (10%)
  between operations  0.65 us (1%)
    pallas_call x1, Pallas kernels, on_device(): pl.pallas_call(functools.partial(kernel, sizes), out_shape=(out,) * 4, in...  42 us
    unnamed x10, local copies, waits for them, and re-layouts  4.84 us

profile of v1, /device:TPU:0, one launch (start us, length us, event | category | flops | bytes accessed | tf_op | source)
XLA Modules:
  0.0 47.5 jit_solution(14912973864134850911)
XLA Ops:
  0.6 42.0 %shard_map.93 = (bf16[1,192,1024]{2,1,0:T(8,128)(2,1)}, bf16[1,192,1024]{2,1,0:T(8,128)(2,1)}, bf16[1,192,1024]{2,1,0:T(8,128)(2,1)}, bf16[1,192,1024]{2,1,0:T(8,128)(2,1)}) custom-call(bf16[1,192,1024]{2,1,0:T(8,128)(2,1)} %q_hbm.1, bf16[1,192,1024]{2,1,0:T(8,128)(2,1)} %k_hbm.1, bf16[1,192,1024]{2,1,0:T(8,128)(2,1)} %v_hbm.1, bf16[1,192,1024]{2,1,0:T(8,128)(2,1)} %x_hbm.1, ...), custom_call_target="tpu_custom_call" | custom-call | tf_op jit(solution)/shard_map/pallas_call | solution.py:325
  42.6 0.0 copy-start.2
  42.6 1.8 %copy.14 = bf16[1,192,1024]{2,1,0:T(8,128)(2,1)} copy(bf16[1,192,1024]{2,1,0:T(8,128)(2,1)} %get-tuple-element.8) | data formatting | bytes 786432
  44.4 0.0 copy-done.2
  44.4 0.0 copy-start.1
  44.4 0.7 %copy.15 = bf16[1,192,1024]{2,1,0:T(8,128)(2,1)} copy(bf16[1,192,1024]{2,1,0:T(8,128)(2,1)S(1)} %copy-done.2) | data formatting | bytes 786432
  45.2 0.4 copy-done.1
  45.6 0.0 copy-start
  45.6 0.7 %copy.16 = bf16[1,192,1024]{2,1,0:T(8,128)(2,1)} copy(bf16[1,192,1024]{2,1,0:T(8,128)(2,1)S(1)} %copy-done.1) | data formatting | bytes 786432
  46.3 0.4 copy-done
  46.7 0.7 %copy.17 = bf16[1,192,1024]{2,1,0:T(8,128)(2,1)} copy(bf16[1,192,1024]{2,1,0:T(8,128)(2,1)S(1)} %copy-done) | data formatting | bytes 786432
Async XLA Ops:
  42.6 1.8 %copy-start.2 = (bf16[1,192,1024]{2,1,0:T(8,128)(2,1)S(1)}, bf16[1,192,1024]{2,1,0:T(8,128)(2,1)}, u32[]{:S(2)}) copy-start(bf16[1,192,1024]{2,1,0:T(8,128)(2,1)} %get-tuple-element.9) | copy-start | bytes 1179652
  44.4 1.1 %copy-start.1 = (bf16[1,192,1024]{2,1,0:T(8,128)(2,1)S(1)}, bf16[1,192,1024]{2,1,0:T(8,128)(2,1)}, u32[]{:S(2)}) copy-start(bf16[1,192,1024]{2,1,0:T(8,128)(2,1)} %get-tuple-element.10) | copy-start | bytes 1179652
  45.6 1.1 %copy-start = (bf16[1,192,1024]{2,1,0:T(8,128)(2,1)S(1)}, bf16[1,192,1024]{2,1,0:T(8,128)(2,1)}, u32[]{:S(2)}) copy-start(bf16[1,192,1024]{2,1,0:T(8,128)(2,1)} %get-tuple-element.11) | copy-start | bytes 1179652

commit v2 on v1

--- a/solution.py
+++ b/solution.py
@@ -10,6 +10,8 @@
 HEAD = 128
 LANES = 128
 EPSILON = 1e-06
+GROUP = 2
+VMEM_LIMIT = 24 << 20
 MESH = pl.DeviceIdType.MESH
 F32 = jnp.float32
 BF16 = jnp.bfloat16
@@ -22,17 +24,21 @@
 def kernel(
     sizes,
     q_hbm, k_hbm, v_hbm, x_hbm, top_hbm, gain_hbm,
-    sec_hbm, qg_hbm, kg_hbm, vg_hbm,
-    q, k, v, x, top, gain, sec, qg, kg, vg,
+    outs,
+    q, k, v, x, top, gain,
     pre_in, pre_out, suf_in, suf_out, states, scores, att, ng, gate, ag, b_out, b_in,
     rows_out, rows_in, inv_out, inv_in,
-    in_sem, sec_sem, out_sem, pre_send, pre_recv, suf_send, suf_recv,
+    in_sem, pre_send, pre_recv, suf_send, suf_recv,
     b_send, b_recv, row_send, row_recv, inv_send, inv_recv,
 ):
     layers, blocks, shards = sizes
-    p, c, t = lax.axis_index("pp"), lax.axis_index("cp"), lax.axis_index("tp")
+    p = lax.axis_index("pp") if layers > 1 else jnp.int32(0)
+    c = lax.axis_index("cp") if blocks > 1 else jnp.int32(0)
+    t = lax.axis_index("tp") if shards > 1 else jnp.int32(0)
     rows, width = q.shape
+    sec, qg, kg, vg = (outs.at[i] for i in range(4))
     heads = width // HEAD
+    groups = [range(h, min(h + GROUP, heads)) for h in range(0, heads, GROUP)]
     padded = rows_out.shape[2]
     total_width = width * shards
 
@@ -143,7 +149,6 @@
     causal = lax.broadcasted_iota(jnp.int32, (rows, rows), 0) >= lax.broadcasted_iota(
         jnp.int32, (rows, rows), 1
     )
-    inner = jnp.logical_and(c > 0, c < blocks - 1)
 
     partners = (shards - 1) + (layers - 1)
     pl.semaphore_wait(
@@ -152,47 +157,51 @@
 
     loads[0].wait()
     loads[1].wait()
-    for h in range(heads):
-        state = dot(k[:, cols(h)], v[:, cols(h)], 0, 0)
-        states[h] = state
+    for group in groups:
+        for h in group:
+            states[h] = dot(k[:, cols(h)], v[:, cols(h)], 0, 0)
         if blocks > 1:
 
             @pl.when(c == 0)
             def _():
-                pre_out[h] = state.astype(BF16)
-                pre_copy(h).start()
+                for h in group:
+                    pre_out[h] = states[h].astype(BF16)
+                    pre_copy(h).start()
 
     for load in loads[2:5]:
         load.wait()
     squares = jnp.zeros((rows, LANES), F32)
-    for h in range(heads):
-        query, value = q[:, cols(h)], v[:, cols(h)]
-        score = jnp.where(causal, dot(query, k[:, cols(h)], 1, 1), 0.0).astype(BF16)
-        scores[h] = score
-        attention = dot(score, value, 1, 0)
-        sig = jax.nn.sigmoid(x[:, cols(h)].astype(F32))
-        gate[:, cols(h)] = sig
-
+    for group in groups:
+        for h in group:
+            query, value = q[:, cols(h)], v[:, cols(h)]
+            score = jnp.where(causal, dot(query, k[:, cols(h)], 1, 1), 0.0).astype(BF16)
+            scores[h] = score
+            att[:, cols(h)] = dot(score, value, 1, 0)
+            gate[:, cols(h)] = jax.nn.sigmoid(x[:, cols(h)].astype(F32))
         if blocks > 1:
 
             @pl.when(c > 0)
             def _():
-                pre_copy(h).wait_recv()
-
-            @pl.when(inner)
-            def _():
-                pre_out[h] = (pre_in[h].astype(F32) + states[h]).astype(BF16)
-                pre_copy(h).start()
-
-        attention = attention + dot(query, pre_in[h], 1, 0)
-        att[:, cols(h)] = attention
-        squares = squares + attention * attention
-        if layers > 1:
-            b_out[h] = (attention * (gain[:, cols(h)] * sig * (1.0 - sig))).astype(BF16)
-            for d in range(1, layers):
-
-                @pl.when(p >= d)
-                def _():
+                for h in group:
+                    pre_copy(h).wait_recv()
+
+                    @pl.when(c < blocks - 1)
+                    def _():
+                        pre_out[h] = (pre_in[h].astype(F32) + states[h]).astype(BF16)
+                        pre_copy(h).start()
+
+        for h in group:
+            attention = att[:, cols(h)] + dot(q[:, cols(h)], pre_in[h], 1, 0)
+            att[:, cols(h)] = attention
+            squares = squares + attention * attention
+            if layers > 1:
+                sig = gate[:, cols(h)]
+                b_out[h] = (attention * (gain[:, cols(h)] * sig * (1.0 - sig))).astype(BF16)
+        for d in range(1, layers):
+
+            @pl.when(p >= d)
+            def _():
+                for h in group:
                     b_copy(d, h).start()
 
     row_start(0, squares)
@@ -215,6 +224,14 @@
     later_inv = [to_col(inv_in[d - 1]) for d in range(1, layers)]
     products = jnp.zeros((rows, LANES), F32)
     for h in range(heads):
+        for d in range(1, layers):
+            if h % GROUP == 0:
+
+                @pl.when(p + d < layers)
+                def _():
+                    for near in range(h, min(h + GROUP, heads)):
+                        b_copy(d, near).wait_recv()
+
         normed = att[:, cols(h)] * inv
         sig = gate[:, cols(h)]
         scaled = gain[:, cols(h)] * sig
@@ -222,10 +239,6 @@
         incoming = top[:, cols(h)].astype(F32)
         for d in range(1, layers):
 
-            @pl.when(p + d < layers)
-            def _():
-                b_copy(d, h).wait_recv()
-
             incoming = incoming * (1.0 + b_in[d - 1, h].astype(F32) * later_inv[d - 1])
         sec[:, cols(h)] = (incoming * factor).astype(BF16)
         normed_grad = incoming * scaled
@@ -234,53 +247,47 @@
         products = products + normed_grad * normed
 
     row_start(1, products)
-    sec_copy = pltpu.make_async_copy(sec, sec_hbm.at[0], sec_sem)
-    sec_copy.start()
     mean = to_col(row_finish(1) / total_width)
-    for h in range(heads):
-        grad = ((ng[:, cols(h)] - att[:, cols(h)] * mean) * inv).astype(BF16)
-        ag[:, cols(h)] = grad
-        state = dot(q[:, cols(h)], grad, 0, 0)
-        states[h] = state
+    for group in groups:
+        for h in group:
+            grad = ((ng[:, cols(h)] - att[:, cols(h)] * mean) * inv).astype(BF16)
+            ag[:, cols(h)] = grad
+            states[h] = dot(q[:, cols(h)], grad, 0, 0)
         if blocks > 1:
 
             @pl.when(c == blocks - 1)
             def _():
-                suf_out[h] = state.astype(BF16)
-                suf_copy(h).start()
-
-    def out_copies(h):
-        return [
-            pltpu.make_async_copy(
-                src.at[:, cols(h)], dst.at[0, :, cols(h)], out_sem.at[i, h]
-            )
-            for i, (src, dst) in enumerate(((qg, qg_hbm), (kg, kg_hbm), (vg, vg_hbm)))
-        ]
-
-    for h in range(heads):
-        query, key, value = q[:, cols(h)], k[:, cols(h)], v[:, cols(h)]
-        grad = ag[:, cols(h)]
-        score_grad = jnp.where(causal, dot(grad, value, 1, 1), 0.0).astype(BF16)
-        query_grad = dot(score_grad, key, 1, 0) + dot(grad, pre_in[h], 1, 1)
-        qg[:, cols(h)] = query_grad.astype(BF16)
-        key_grad = dot(score_grad, query, 0, 0)
-        value_grad = dot(scores[h], grad, 0, 0)
+                for h in group:
+                    suf_out[h] = states[h].astype(BF16)
+                    suf_copy(h).start()
+
+    for group in groups:
+        for h in group:
+            query, key, value = q[:, cols(h)], k[:, cols(h)], v[:, cols(h)]
+            grad = ag[:, cols(h)]
+            score_grad = jnp.where(causal, dot(grad, value, 1, 1), 0.0).astype(BF16)
+            query_grad = dot(score_grad, key, 1, 0) + dot(grad, pre_in[h], 1, 1)
+            qg[:, cols(h)] = query_grad.astype(BF16)
+            att[:, cols(h)] = dot(score_grad, query, 0, 0)
+            ng[:, cols(h)] = dot(scores[h], grad, 0, 0)
         if blocks > 1:
 
             @pl.when(c < blocks - 1)
             def _():
-                suf_copy(h).wait_recv()
-
-            @pl.when(inner)
-            def _():
-                suf_out[h] = (suf_in[h].astype(F32) + states[h]).astype(BF16)
-                suf_copy(h).start()
-
-        suffix = suf_in[h]
-        kg[:, cols(h)] = (key_grad + dot(value, suffix, 1, 1)).astype(BF16)
-        vg[:, cols(h)] = (value_grad + dot(key, suffix, 1, 0)).astype(BF16)
-        for copy in out_copies(h):
-            copy.start()
+                for h in group:
+                    suf_copy(h).wait_recv()
+
+                    @pl.when(c > 0)
+                    def _():
+                        suf_out[h] = (suf_in[h].astype(F32) + states[h]).astype(BF16)
+                        suf_copy(h).start()
+
+        for h in group:
+            suffix = suf_in[h]
+            key_grad = att[:, cols(h)] + dot(v[:, cols(h)], suffix, 1, 1)
+            kg[:, cols(h)] = key_grad.astype(BF16)
+            value_grad = ng[:, cols(h)] + dot(k[:, cols(h)], suffix, 1, 0)
+            vg[:, cols(h)] = value_grad.astype(BF16)
 
     if blocks > 1:
 
@@ -305,10 +312,17 @@
     for i in range(2):
         for d in range(1, shards):
             row_copy(i, d).wait_send()
-    sec_copy.wait()
-    for h in range(heads):
-        for copy in out_copies(h):
-            copy.wait()
+
+
+def write_kernel(outs, sec_hbm, qg_hbm, kg_hbm, vg_hbm, sem):
+    copies = [
+        pltpu.make_async_copy(outs.at[i], dst.at[0], sem.at[i])
+        for i, dst in enumerate((sec_hbm, qg_hbm, kg_hbm, vg_hbm))
+    ]
+    for copy in copies:
+        copy.start()
+    for copy in copies:
+        copy.wait()
 
 
 def on_device(sizes, q, k, v, x, top, gains):
@@ -322,14 +336,16 @@
     square = pltpu.VMEM((heads, HEAD, HEAD), BF16)
     dma = pltpu.SemaphoreType.DMA
     out = jax.ShapeDtypeStruct((1, rows, width), BF16)
-    return pl.pallas_call(
+    q, k, v, x, top, gains = (
+        pltpu.with_memory_space_constraint(a, pltpu.HBM) for a in (q, k, v, x, top, gains)
+    )
+    outs = pl.pallas_call(
         functools.partial(kernel, sizes),
-        out_shape=(out,) * 4,
-        in_specs=[pl.BlockSpec(memory_space=pl.ANY)] * 6,
-        out_specs=(pl.BlockSpec(memory_space=pl.ANY),) * 4,
+        out_shape=jax.ShapeDtypeStruct((4, rows, width), BF16),
+        in_specs=[pl.BlockSpec(memory_space=pltpu.HBM)] * 6,
+        out_specs=pl.BlockSpec(memory_space=pltpu.VMEM),
         scratch_shapes=[
             wide, wide, wide, wide, wide, pltpu.VMEM((1, width), F32),
-            wide, wide, wide, wide,
             square, square, square, square,
             pltpu.VMEM((heads, HEAD, HEAD), F32),
             pltpu.VMEM((heads, rows, rows), BF16),
@@ -340,14 +356,22 @@
             pltpu.VMEM((2, peers, 8, padded), F32),
             pltpu.VMEM((8, padded), F32),
             pltpu.VMEM((others, 8, padded), F32),
-            dma((6,)), dma, dma((3, heads)),
+            dma((6,)),
             dma((heads,)), dma((heads,)), dma((heads,)), dma((heads,)),
             dma((others, heads)), dma((others, heads)),
             dma((2, peers)), dma((2, peers)),
             dma((others,)), dma((others,)),
         ],
-        compiler_params=pltpu.CompilerParams(collective_id=0, has_side_effects=True),
+        compiler_params=pltpu.CompilerParams(collective_id=0, has_side_effects=True, vmem_limit_bytes=VMEM_LIMIT),
     )(q, k, v, x, top, gains)
+    return pl.pallas_call(
+        write_kernel,
+        out_shape=(out,) * 4,
+        in_specs=[pl.BlockSpec(memory_space=pltpu.VMEM)],
+        out_specs=(pl.BlockSpec(memory_space=pl.ANY),) * 4,
+        scratch_shapes=[dma((4,))],
+        compiler_params=pltpu.CompilerParams(vmem_limit_bytes=1 << 20),
+    )(outs)
 
 
 def solution(mesh):

time: 47.7 us -> 43.3 us (0.908)
  local copies, waits for them, and re-layouts: 4.84 us -> 0 us
  Pallas kernels: 42 us -> 42.6 us
    unnamed x10 -> x0, local copies, waits for them, and re-layouts: 4.84 us -> none
    pallas_call x1 -> x2, Pallas kernels: 42 us -> 42.6 us  [the longest x1 41.4 us: on_device(): pl.pallas_call(functools.partial(kernel, sizes), out_shape=jax.ShapeDtype...]
where the time goes in v2:
time: 43.3 us; the launch traced here: 43.2 us
  Pallas kernels  42.6 us (98%)
  between operations  0.64 us (1%)
    pallas_call x1, Pallas kernels, on_device(): pl.pallas_call(functools.partial(kernel, sizes), out_shape=jax.ShapeDtype...  41.4 us
    pallas_call x1, Pallas kernels, on_device(): pl.pallas_call(write_kernel, out_shape=(out,) * 4, in_specs=[pl.BlockSpec...  1.17 us

profile of v2, /device:TPU:0, one launch (start us, length us, event | category | flops | bytes accessed | tf_op | source)
XLA Modules:
  0.0 43.2 jit_solution(3035080363008990)
XLA Ops:
  0.6 41.4 %shard_map.93.outs = bf16[4,192,1024]{2,1,0:T(8,128)(2,1)S(1)} custom-call(bf16[1,192,1024]{2,1,0:T(8,128)(2,1)} %q_hbm.1, bf16[1,192,1024]{2,1,0:T(8,128)(2,1)} %k_hbm.1, bf16[1,192,1024]{2,1,0:T(8,128)(2,1)} %v_hbm.1, bf16[1,192,1024]{2,1,0:T(8,128)(2,1)} %x_hbm.1, bf16[192,1024]{1,0:T(8,128)(2,1)} %top_hbm.1, f32[1,1024]{1,0:T(1,128)} %gain_hbm.1), custom_call_target="tpu_custom_call" | custom-call | tf_op jit(solution)/shard_map/pallas_call | solution.py:342
  42.0 1.2 %shard_map.94 = (bf16[1,192,1024]{2,1,0:T(8,128)(2,1)}, bf16[1,192,1024]{2,1,0:T(8,128)(2,1)}, bf16[1,192,1024]{2,1,0:T(8,128)(2,1)}, bf16[1,192,1024]{2,1,0:T(8,128)(2,1)}) custom-call(bf16[4,192,1024]{2,1,0:T(8,128)(2,1)S(1)} %shard_map.93.outs), custom_call_target="tpu_custom_call" | custom-call | tf_op jit(solution)/shard_map/pallas_call | solution.py:367

commit v3 on v2

--- a/solution.py
+++ b/solution.py
@@ -11,6 +11,7 @@
 LANES = 128
 EPSILON = 1e-06
 GROUP = 2
+PIECES = 1
 VMEM_LIMIT = 24 << 20
 MESH = pl.DeviceIdType.MESH
 F32 = jnp.float32
@@ -42,6 +43,12 @@
     padded = rows_out.shape[2]
     total_width = width * shards
 
+    def part(i):
+        return slice(i * (HEAD // PIECES), (i + 1) * (HEAD // PIECES))
+
+    def pieces(group):
+        return [(h, i) for h in group for i in range(PIECES)]
+
     def cols(h):
         return slice(h * HEAD, (h + 1) * HEAD)
 
@@ -53,7 +60,7 @@
         pltpu.make_async_copy(gain_hbm, gain, in_sem.at[4]),
         pltpu.make_async_copy(top_hbm, top, in_sem.at[5]),
     ]
-    for load in loads:
+    for load in loads[:2]:
         load.start()
 
     barrier = pltpu.get_barrier_semaphore()
@@ -90,17 +97,17 @@
             b_in[d - 1] = jnp.zeros(b_in.shape[1:], b_in.dtype)
             inv_in[d - 1] = jnp.zeros(inv_in.shape[1:], inv_in.dtype)
 
-    def pre_copy(h):
+    def pre_copy(h, i):
         return pltpu.make_async_remote_copy(
-            src_ref=pre_out.at[h], dst_ref=pre_in.at[h],
-            send_sem=pre_send.at[h], recv_sem=pre_recv.at[h],
+            src_ref=pre_out.at[h, part(i)], dst_ref=pre_in.at[h, part(i)],
+            send_sem=pre_send.at[h, i], recv_sem=pre_recv.at[h, i],
             device_id={"cp": c + 1}, device_id_type=MESH,
         )
 
-    def suf_copy(h):
+    def suf_copy(h, i):
         return pltpu.make_async_remote_copy(
-            src_ref=suf_out.at[h], dst_ref=suf_in.at[h],
-            send_sem=suf_send.at[h], recv_sem=suf_recv.at[h],
+            src_ref=suf_out.at[h, part(i)], dst_ref=suf_in.at[h, part(i)],
+            send_sem=suf_send.at[h, i], recv_sem=suf_recv.at[h, i],
             device_id={"cp": c - 1}, device_id_type=MESH,
         )
 
@@ -134,8 +141,12 @@
     def to_col(row):
         return jnp.broadcast_to(row[0:1], (LANES, padded)).T[:rows]
 
-    def row_start(i, partial):
-        rows_out[i] = to_row(partial)
+    def row_start(i, partials):
+        ids = lax.broadcasted_iota(jnp.int32, (8, padded), 0)
+        packed = to_row(partials[0])
+        for j in range(1, len(partials)):
+            packed = jnp.where(ids == j, to_row(partials[j]), packed)
+        rows_out[i] = packed
         for d in range(1, shards):
             row_copy(i, d).start()
 
@@ -157,6 +168,8 @@
 
     loads[0].wait()
     loads[1].wait()
+    for load in loads[2:]:
+        load.start()
     for group in groups:
         for h in group:
             states[h] = dot(k[:, cols(h)], v[:, cols(h)], 0, 0)
@@ -165,12 +178,15 @@
             @pl.when(c == 0)
             def _():
                 for h in group:
-                    pre_out[h] = states[h].astype(BF16)
-                    pre_copy(h).start()
-
-    for load in loads[2:5]:
+                    for i in range(PIECES):
+                        pre_out[h, part(i)] = states[h, part(i)].astype(BF16)
+                        pre_copy(h, i).start()
+
+    for load in loads[2:]:
         load.wait()
+    merged = layers <= 2
     squares = jnp.zeros((rows, LANES), F32)
+    firsts = jnp.zeros((rows, LANES), F32)
     for group in groups:
         for h in group:
             query, value = q[:, cols(h)], v[:, cols(h)]
@@ -182,20 +198,25 @@
 
             @pl.when(c > 0)
             def _():
-                for h in group:
-                    pre_copy(h).wait_recv()
+                for h, i in pieces(group):
+                    pre_copy(h, i).wait_recv()
 
                     @pl.when(c < blocks - 1)
                     def _():
-                        pre_out[h] = (pre_in[h].astype(F32) + states[h]).astype(BF16)
-                        pre_copy(h).start()
+                        total = pre_in[h, part(i)].astype(F32) + states[h, part(i)]
+                        pre_out[h, part(i)] = total.astype(BF16)
+                        pre_copy(h, i).start()
 
         for h in group:
             attention = att[:, cols(h)] + dot(q[:, cols(h)], pre_in[h], 1, 0)
             att[:, cols(h)] = attention
             squares = squares + attention * attention
+            sig = gate[:, cols(h)]
+            if merged:
+                weighted = top[:, cols(h)].astype(F32) * (gain[:, cols(h)] * sig)
+                ng[:, cols(h)] = weighted
+                firsts = firsts + weighted * attention
             if layers > 1:
-                sig = gate[:, cols(h)]
                 b_out[h] = (attention * (gain[:, cols(h)] * sig * (1.0 - sig))).astype(BF16)
         for d in range(1, layers):
 
@@ -204,10 +225,10 @@
                 for h in group:
                     b_copy(d, h).start()
 
-    row_start(0, squares)
-    loads[5].wait()
-    inv_row = 1.0 / jnp.sqrt(row_finish(0) / total_width + EPSILON)
-    inv_out[...] = inv_row
+    row_start(0, (squares, firsts))
+    sums = row_finish(0)
+    inv_row = 1.0 / jnp.sqrt(sums[0:1] / total_width + EPSILON)
+    inv_out[...] = jnp.broadcast_to(inv_row, inv_out.shape)
     for d in range(1, layers):
 
         @pl.when(p >= d)
@@ -215,42 +236,72 @@
             inv_copy(d).start()
 
     inv = to_col(inv_row)
-    for d in range(1, layers):
-
-        @pl.when(p + d < layers)
-        def _():
-            inv_copy(d).wait_recv()
-
-    later_inv = [to_col(inv_in[d - 1]) for d in range(1, layers)]
-    products = jnp.zeros((rows, LANES), F32)
-    for h in range(heads):
+
+    def wait_inv():
         for d in range(1, layers):
-            if h % GROUP == 0:
-
-                @pl.when(p + d < layers)
-                def _():
-                    for near in range(h, min(h + GROUP, heads)):
-                        b_copy(d, near).wait_recv()
-
-        normed = att[:, cols(h)] * inv
-        sig = gate[:, cols(h)]
-        scaled = gain[:, cols(h)] * sig
-        factor = 1.0 + normed * scaled * (1.0 - sig)
+
+            @pl.when(p + d < layers)
+            def _():
+                inv_copy(d).wait_recv()
+
+    def wait_b(group):
+        for d in range(1, layers):
+
+            @pl.when(p + d < layers)
+            def _():
+                for h in group:
+                    b_copy(d, h).wait_recv()
+
+    def later(h, later_inv):
         incoming = top[:, cols(h)].astype(F32)
         for d in range(1, layers):
-
             incoming = incoming * (1.0 + b_in[d - 1, h].astype(F32) * later_inv[d - 1])
-        sec[:, cols(h)] = (incoming * factor).astype(BF16)
-        normed_grad = incoming * scaled
-        ng[:, cols(h)] = normed_grad
-        att[:, cols(h)] = normed
-        products = products + normed_grad * normed
-
-    row_start(1, products)
-    mean = to_col(row_finish(1) / total_width)
+        return incoming
+
+    if merged:
+        mean_row = sums[1:2]
+        if layers > 1:
+            seconds = jnp.zeros((rows, LANES), F32)
+            for group in groups:
+                wait_b(group)
+                for h in group:
+                    seconds = seconds + ng[:, cols(h)] * att[:, cols(h)] * b_in[0, h].astype(F32)
+
+            @pl.when(p < layers - 1)
+            def _():
+                row_start(1, (seconds,))
+                wait_inv()
+                total = row_finish(1)
+                for d in range(1, shards):
+                    row_copy(1, d).wait_send()
+                rows_out[1] = total
+
+            @pl.when(p == layers - 1)
+            def _():
+                rows_out[1] = jnp.zeros(rows_out.shape[1:], F32)
+
+            mean_row = mean_row + inv_in[0, 0:1] * rows_out[1, 0:1]
+        mean_row = mean_row * inv_row
+        later_inv = [to_col(inv_in[d - 1]) for d in range(1, layers)]
+    else:
+        wait_inv()
+        later_inv = [to_col(inv_in[d - 1]) for d in range(1, layers)]
+        products = jnp.zeros((rows, LANES), F32)
+        for group in groups:
+            wait_b(group)
+            for h in group:
+                weighted = later(h, later_inv) * (gain[:, cols(h)] * gate[:, cols(h)])
+                ng[:, cols(h)] = weighted
+                products = products + weighted * att[:, cols(h)] * inv
+        row_start(1, (products,))
+        mean_row = row_finish(1)
+    mean = to_col(mean_row / total_width)
     for group in groups:
         for h in group:
-            grad = ((ng[:, cols(h)] - att[:, cols(h)] * mean) * inv).astype(BF16)
+            weighted = ng[:, cols(h)]
+            if merged and layers > 1:
+                weighted = weighted * (1.0 + b_in[0, h].astype(F32) * later_inv[0])
+            grad = ((weighted - att[:, cols(h)] * inv * mean) * inv).astype(BF16)
             ag[:, cols(h)] = grad
             states[h] = dot(q[:, cols(h)], grad, 0, 0)
         if blocks > 1:
@@ -258,11 +309,16 @@
             @pl.when(c == blocks - 1)
             def _():
                 for h in group:
-                    suf_out[h] = states[h].astype(BF16)
-                    suf_copy(h).start()
+                    for i in range(PIECES):
+                        suf_out[h, part(i)] = states[h, part(i)].astype(BF16)
+                        suf_copy(h, i).start()
 
     for group in groups:
         for h in group:
+            sig = gate[:, cols(h)]
+            slope = gain[:, cols(h)] * sig * (1.0 - sig)
+            factor = 1.0 + att[:, cols(h)] * inv * slope
+            sec[:, cols(h)] = (later(h, later_inv) * factor).astype(BF16)
             query, key, value = q[:, cols(h)], k[:, cols(h)], v[:, cols(h)]
             grad = ag[:, cols(h)]
             score_grad = jnp.where(causal, dot(grad, value, 1, 1), 0.0).astype(BF16)
@@ -274,13 +330,14 @@
 
             @pl.when(c < blocks - 1)
             def _():
-                for h in group:
-                    suf_copy(h).wait_recv()
+                for h, i in pieces(group):
+                    suf_copy(h, i).wait_recv()
 
                     @pl.when(c > 0)
                     def _():
-                        suf_out[h] = (suf_in[h].astype(F32) + states[h]).astype(BF16)
-                        suf_copy(h).start()
+                        total = suf_in[h, part(i)].astype(F32) + states[h, part(i)]
+                        suf_out[h, part(i)] = total.astype(BF16)
+                        suf_copy(h, i).start()
 
         for h in group:
             suffix = suf_in[h]
@@ -293,13 +350,13 @@
 
         @pl.when(c < blocks - 1)
         def _():
-            for h in range(heads):
-                pre_copy(h).wait_send()
+            for h, i in pieces(range(heads)):
+                pre_copy(h, i).wait_send()
 
         @pl.when(c > 0)
         def _():
-            for h in range(heads):
-                suf_copy(h).wait_send()
+            for h, i in pieces(range(heads)):
+                suf_copy(h, i).wait_send()
 
     for d in range(1, layers):
 
@@ -309,9 +366,11 @@
             for h in range(heads):
                 b_copy(d, h).wait_send()
 
-    for i in range(2):
+    for d in range(1, shards):
+        row_copy(0, d).wait_send()
+    if not merged:
         for d in range(1, shards):
-            row_copy(i, d).wait_send()
+            row_copy(1, d).wait_send()
 
 
 def write_kernel(outs, sec_hbm, qg_hbm, kg_hbm, vg_hbm, sem):
@@ -335,6 +394,7 @@
     wide32 = pltpu.VMEM((rows, width), F32)
     square = pltpu.VMEM((heads, HEAD, HEAD), BF16)
     dma = pltpu.SemaphoreType.DMA
+    chain = dma((heads, PIECES))
     out = jax.ShapeDtypeStruct((1, rows, width), BF16)
     q, k, v, x, top, gains = (
         pltpu.with_memory_space_constraint(a, pltpu.HBM) for a in (q, k, v, x, top, gains)
@@ -357,7 +417,7 @@
             pltpu.VMEM((8, padded), F32),
             pltpu.VMEM((others, 8, padded), F32),
             dma((6,)),
-            dma((heads,)), dma((heads,)), dma((heads,)), dma((heads,)),
+            chain, chain, chain, chain,
             dma((others, heads)), dma((others, heads)),
             dma((2, peers)), dma((2, peers)),
             dma((others,)), dma((others,)),

time: 43.3 us -> 42.6 us (0.984)
  Pallas kernels: 42.6 us -> 41.8 us
    pallas_call x1, Pallas kernels: 41.4 us -> 40.6 us  [on_device(): pl.pallas_call(functools.partial(kernel, sizes), out_shape=jax.ShapeDtype...]
where the time goes in v3:
time: 42.6 us; the launch traced here: 42.4 us
  Pallas kernels  41.8 us (98%)
  between operations  0.64 us (2%)
    pallas_call x1, Pallas kernels, on_device(): pl.pallas_call(functools.partial(kernel, sizes), out_shape=jax.ShapeDtype...  40.6 us
    pallas_call x1, Pallas kernels, on_device(): pl.pallas_call(write_kernel, out_shape=(out,) * 4, in_specs=[pl.BlockSpec...  1.17 us

profile of v3, /device:TPU:0, one launch (start us, length us, event | category | flops | bytes accessed | tf_op | source)
XLA Modules:
  0.0 42.4 jit_solution(11789997962317470716)
XLA Ops:
  0.6 40.6 %shard_map.93.outs = bf16[4,192,1024]{2,1,0:T(8,128)(2,1)S(1)} custom-call(bf16[1,192,1024]{2,1,0:T(8,128)(2,1)} %q_hbm.1, bf16[1,192,1024]{2,1,0:T(8,128)(2,1)} %k_hbm.1, bf16[1,192,1024]{2,1,0:T(8,128)(2,1)} %v_hbm.1, bf16[1,192,1024]{2,1,0:T(8,128)(2,1)} %x_hbm.1, bf16[192,1024]{1,0:T(8,128)(2,1)} %top_hbm.1, f32[1,1024]{1,0:T(1,128)} %gain_hbm.1), custom_call_target="tpu_custom_call" | custom-call | tf_op jit(solution)/shard_map/pallas_call | solution.py:402
  41.2 1.2 %shard_map.94 = (bf16[1,192,1024]{2,1,0:T(8,128)(2,1)}, bf16[1,192,1024]{2,1,0:T(8,128)(2,1)}, bf16[1,192,1024]{2,1,0:T(8,128)(2,1)}, bf16[1,192,1024]{2,1,0:T(8,128)(2,1)}) custom-call(bf16[4,192,1024]{2,1,0:T(8,128)(2,1)S(1)} %shard_map.93.outs), custom_call_target="tpu_custom_call" | custom-call | tf_op jit(solution)/shard_map/pallas_call | solution.py:427

commit v4 on v3

--- a/solution.py
+++ b/solution.py
@@ -10,7 +10,7 @@
 HEAD = 128
 LANES = 128
 EPSILON = 1e-06
-GROUP = 2
+GROUP = 1
 PIECES = 1
 VMEM_LIMIT = 24 << 20
 MESH = pl.DeviceIdType.MESH

time: 42.6 us -> 41.3 us (0.969)
  Pallas kernels: 41.8 us -> 40.5 us
    pallas_call x1, Pallas kernels: 40.6 us -> 39.3 us  [on_device(): pl.pallas_call(functools.partial(kernel, sizes), out_shape=jax.ShapeDtype...]
where the time goes in v4:
time: 41.3 us; the launch traced here: 41.2 us
  Pallas kernels  40.5 us (98%)
  between operations  0.64 us (2%)
    pallas_call x1, Pallas kernels, on_device(): pl.pallas_call(functools.partial(kernel, sizes), out_shape=jax.ShapeDtype...  39.3 us
    pallas_call x1, Pallas kernels, on_device(): pl.pallas_call(write_kernel, out_shape=(out,) * 4, in_specs=[pl.BlockSpec...  1.17 us

profile of v4, /device:TPU:0, one launch (start us, length us, event | category | flops | bytes accessed | tf_op | source)
XLA Modules:
  0.0 41.2 jit_solution(5003040962653061175)
XLA Ops:
  0.6 39.3 %shard_map.93.outs = bf16[4,192,1024]{2,1,0:T(8,128)(2,1)S(1)} custom-call(bf16[1,192,1024]{2,1,0:T(8,128)(2,1)} %q_hbm.1, bf16[1,192,1024]{2,1,0:T(8,128)(2,1)} %k_hbm.1, bf16[1,192,1024]{2,1,0:T(8,128)(2,1)} %v_hbm.1, bf16[1,192,1024]{2,1,0:T(8,128)(2,1)} %x_hbm.1, bf16[192,1024]{1,0:T(8,128)(2,1)} %top_hbm.1, f32[1,1024]{1,0:T(1,128)} %gain_hbm.1), custom_call_target="tpu_custom_call" | custom-call | tf_op jit(solution)/shard_map/pallas_call | solution.py:402
  40.0 1.2 %shard_map.94 = (bf16[1,192,1024]{2,1,0:T(8,128)(2,1)}, bf16[1,192,1024]{2,1,0:T(8,128)(2,1)}, bf16[1,192,1024]{2,1,0:T(8,128)(2,1)}, bf16[1,192,1024]{2,1,0:T(8,128)(2,1)}) custom-call(bf16[4,192,1024]{2,1,0:T(8,128)(2,1)S(1)} %shard_map.93.outs), custom_call_target="tpu_custom_call" | custom-call | tf_op jit(solution)/shard_map/pallas_call | solution.py:427
